TPU v7x, 32 devices: a whole 2x2x4 slice. The times are simulated.
32 devices in a mesh: parts: 2 (over y), seq: 4 (over z), tok: 2 (over x), head: 2 (over core).
Axes of the slice: x: 2, y: 2, z: 4, core: 2. Of those that a mesh axis runs over, the one named last changes fastest.
Arguments:
- values: bfloat16 [8192, 2048], P(('parts', 'seq', 'tok'), 'head'), parts along dimension 0, may hold values from -6 to 6
- key_rows: bfloat16 [8192, 128], P(('parts', 'seq', 'tok')), parts along dimension 0, may hold values from -0.5 to 0.5
- query_rows: bfloat16 [8192, 128], P(('parts', 'seq', 'tok')), parts along dimension 0, may hold values from -6 to 6
- decay_codes: int32 [32, 8192], P('head', ('parts', 'seq', 'tok')), parts along dimension 1, may hold values from 0 to 48398, as said below
- weight_codes: int32 [12, 32, 8192], P(None, 'head', ('parts', 'seq', 'tok')), parts along dimension 2, may hold values from 16 to 511
- norm_gain: float32 [2048], P('head'), may hold values from 0.5 to 1.5
Outputs:
- mixed: bfloat16 [8192, 2048], P(('parts', 'seq', 'tok'), 'head'), parts along dimension 0
There are 2 independent parts, one for each index of `parts`. A program takes and returns all parts, laid end to end along the dimension named above; an argument that names none is the same for every part. Nothing has to cross between parts.
Inputs may be any that keep to these rules, and one draw needn't show every extreme that they name: `decay_codes`: Log-decay numerators over 65536. `weight_codes`: level weight numerators over 256.
All inputs are finite; a program needn't handle non-finite values.
Results may differ from a plain program's by a relative error of at most 0.0048.
Values sent between devices are 32-bit elements; how exact they have to be, the bound alone decides.
A program may use at most 64 MiB of HBM per device.

v0:
```python
import jax
import jax.numpy as jnp
from jax import lax
from jax.sharding import PartitionSpec as P

BUCKET = 64


decay_denominator = 65536.0
weight_denominator = 256.0
norm_epsilon = 1e-05
row_limit = 512
highest = lax.Precision.HIGHEST


def from_partner(value, axis, distance):
    mask = 2**distance
    pairs = [(source, source ^ mask) for source in range(lax.axis_size(axis))]
    return lax.ppermute(value, axis, pairs)


def bit_count(numbers, width_bits):
    result = jnp.zeros(numbers.shape, jnp.int32)
    for bit_place in range(width_bits):
        result = result + (numbers >= 1 << bit_place).astype(jnp.int32)
    return result


def token_spread(levels_full, lam_rows, slot_count):
    spread = jnp.zeros(levels_full.shape, jnp.float32)
    for slot in range(slot_count):
        spread = spread + jnp.where(levels_full == slot, lam_rows[slot][:, None], 0.0)
    return spread


def decay_sums(decay_codes):
    return jnp.cumsum(-decay_codes.astype(jnp.float32) / decay_denominator, axis=1)


def near_terms(values, key_rows, query_rows, cumulative, level_scale, head_size):
    token_count = values.shape[0]
    head_count = cumulative.shape[0]
    buckets = token_count // BUCKET
    level_bits = (buckets - 1).bit_length()
    bucket_ids = jnp.arange(buckets, dtype=jnp.int32)
    levels = bit_count(jnp.bitwise_xor(bucket_ids[:, None], bucket_ids[None, :]), level_bits)
    head_weights = jnp.transpose(level_scale[: level_bits + 1], (1, 0, 2))
    block_rows = min(row_limit, token_count)
    scores = jnp.einsum("tn,sn->ts", query_rows, key_rows, preferred_element_type=jnp.float32)
    causal = jnp.arange(0, block_rows)[:, None] >= jnp.arange(block_rows)[None, :]
    levels_full = jnp.broadcast_to(
        levels[:, None, :, None], (block_rows // BUCKET, BUCKET, block_rows // BUCKET, BUCKET)
    ).reshape(block_rows, block_rows)

    def one_head(head_item):
        cum_rates, weights, head_index = head_item
        log_gap = jnp.where(
            causal, cum_rates[0:block_rows, None] - cum_rates[None, :block_rows], 0.0
        )
        spread = token_spread(levels_full, weights, level_bits + 1)
        mixing = jnp.where(causal, jnp.exp(log_gap) * spread * scores, 0.0).astype(jnp.bfloat16)
        columns = lax.dynamic_slice_in_dim(values, head_index * head_size, head_size, 1)
        return jnp.dot(mixing, columns, preferred_element_type=jnp.float32)

    pieces = lax.map(one_head, (cumulative, head_weights, jnp.arange(head_count, dtype=jnp.int32)))
    return pieces


def block_state(values, key_rows, cumulative, head_size):
    token_count = values.shape[0]
    head_count = cumulative.shape[0]
    end_decay = jnp.exp(cumulative[:, -1:] - cumulative)
    decayed = (
        values.astype(jnp.float32).reshape(token_count, head_count, head_size)
        * end_decay.T[:, :, None]
    ).astype(jnp.bfloat16)
    return jnp.einsum("tn,thp->hnp", key_rows, decayed, preferred_element_type=jnp.float32)


def decay_coeff(sources, own_index, log_gap):
    earlier = (sources < own_index)[:, None]
    return jnp.where(earlier, jnp.exp(jnp.where(earlier, log_gap, 0.0)), 0.0)


def level_onehot(levels, slot_ids):
    return (levels[:, None] == slot_ids[None, :]).astype(jnp.float32)


def pair_step(aggregate, block_total, prefix, far_levels, slot, partner, partner_total, is_upper):
    weight = jnp.where(is_upper, jnp.exp(prefix), 0.0)
    far_levels = far_levels.at[slot].add(weight[:, None, None] * partner)
    aggregate = jnp.where(
        is_upper,
        jnp.exp(block_total)[:, None, None] * partner + aggregate,
        jnp.exp(partner_total)[:, None, None] * aggregate + partner,
    )
    prefix = jnp.where(is_upper, prefix + partner_total, prefix)
    return (aggregate, block_total + partner_total, prefix, far_levels)


def finish(near, far_levels, far_weights, query_rows, cumulative, norm_gain, head_size):
    token_count = query_rows.shape[0]
    head_count = cumulative.shape[0]
    queries = query_rows.astype(jnp.float32)
    readout = jnp.zeros(near.shape, jnp.float32)
    for slot in range(far_levels.shape[0]):
        part_out = jnp.einsum("tn,hnp->htp", queries, far_levels[slot], precision=highest)
        readout = readout + far_weights[slot][:, :, None] * part_out
    combined = near + jnp.exp(cumulative)[:, :, None] * readout
    inverse_rms = lax.rsqrt(jnp.mean(combined * combined, axis=2, keepdims=True) + norm_epsilon)
    normed = combined * inverse_rms * norm_gain.reshape(head_count, 1, head_size)
    return (
        jnp.transpose(normed, (1, 0, 2))
        .reshape(token_count, head_count * head_size)
        .astype(jnp.bfloat16)
    )


def local(values, key_rows, query_rows, decay_codes, weight_codes, norm_gain):
    head_count = decay_codes.shape[0]
    head_size = values.shape[1] // head_count
    level_scale = weight_codes.astype(jnp.float32) / weight_denominator
    cumulative = decay_sums(decay_codes)
    own_state = block_state(values, key_rows, cumulative, head_size)
    near = near_terms(values, key_rows, query_rows, cumulative, level_scale, head_size)
    base_level = (values.shape[0] // BUCKET).bit_length() - 1
    tok_count = lax.axis_size("tok")
    tok_bits = tok_count.bit_length() - 1
    tok_index = lax.axis_index("tok")
    seq_count = lax.axis_size("seq")
    seq_bits = seq_count.bit_length() - 1
    seq_index = lax.axis_index("seq")
    far_levels = jnp.zeros((tok_bits + seq_bits,) + own_state.shape, jnp.float32)
    aggregate = own_state
    block_total = cumulative[:, -1]
    prefix = jnp.zeros(block_total.shape, jnp.float32)
    for bit_place in range(tok_bits):
        partner, partner_total = from_partner((aggregate, block_total), "tok", bit_place)
        is_upper = tok_index >> bit_place & 1 == 1
        aggregate, block_total, prefix, far_levels = pair_step(
            aggregate, block_total, prefix, far_levels, bit_place, partner, partner_total, is_upper
        )
    totals = lax.all_gather(block_total[None], "seq", axis=0, tiled=True)
    inclusive = jnp.cumsum(totals, axis=0)
    before_me = jnp.sum(
        jnp.where((jnp.arange(seq_count, dtype=jnp.int32) < seq_index)[:, None], totals, 0.0),
        axis=0,
    )
    reach = prefix + before_me
    seq_slots = jnp.arange(1, seq_bits + 1, dtype=jnp.int32)
    shard_piece = lax.all_gather(aggregate[None], "seq", axis=0, tiled=True)
    sources = jnp.arange(shard_piece.shape[0], dtype=jnp.int32)
    coefficient = decay_coeff(sources, seq_index, reach[None, :] - inclusive)
    onehot = level_onehot(bit_count(jnp.bitwise_xor(sources, seq_index), seq_bits), seq_slots)
    added = jnp.einsum("mh,mj,mhnp->jhnp", coefficient, onehot, shard_piece, precision=highest)
    far_levels = far_levels.at[tok_bits:].add(added)
    far_weights = level_scale[base_level + 1 : base_level + 1 + tok_bits + seq_bits]
    return finish(near, far_levels, far_weights, query_rows, cumulative, norm_gain, head_size)


def solution(mesh):
    return jax.shard_map(
        local,
        mesh=mesh,
        in_specs=(
            P(("parts", "seq", "tok"), "head"),
            P(("parts", "seq", "tok"), None),
            P(("parts", "seq", "tok"), None),
            P("head", ("parts", "seq", "tok")),
            P(None, "head", ("parts", "seq", "tok")),
            P("head"),
        ),
        out_specs=P(("parts", "seq", "tok"), "head"),
        check_vma=False,
    )
```

profile of v0, /device:TPU:0, one launch (start us, length us, event | category | flops | bytes accessed | tf_op | source)
XLA Modules:
  0.0 126.6 jit_solution(5198924465103910711)
XLA Ops:
  6.5 0.8 copy_bitcast_fusion.1
  7.4 1.1 reduce-window.6
  9.0 3.0 %collective-permute-start.1 = (f32[16]{0:T(128)S(1)}, f32[16]{0:T(128)S(1)}, u32[]{:S(2)}, u32[]{:S(2)}) collective-permute-start(f32[16]{0:T(128)S(1)} %slice_reduce_fusion.1), channel_id=1, source_target_pairs={{0,2},{2,0},{1,3},{3,1},{4,6},{6,4},{5,7},{7,5},{8,10},{10,8},{9,1... | collective-permute-start | bytes 200 | tf_op jit(solution)/shard_map/ppermute | solution.py:19
  12.1 1.5 %copy.29 = bf16[512,1024]{0,1:T(8,128)(2,1)S(1)} copy(bf16[512,1024]{1,0:T(8,128)(2,1)} %param.12) | data formatting | bytes 2097152 | tf_op args[0]
  14.5 0.8 copy-done.4
  15.3 1.3 %fusion.58 = f32[512,512]{1,0:T(8,128)} fusion(bf16[512,128]{1,0:T(8,128)(2,1)S(1)} %copy-done, bf16[512,128]{1,0:T(8,128)(2,1)S(1)} %copy-done.5), kind=kOutput, calls=%fused_computation.89 | convolution fusion | flops 67108864 | bytes 1310720 | tf_op jit(solution)/shard_map/tn,sn->ts/dot_general | solution.py:49
  17.8 12.4 %all-reduce = f32[64]{0:T(128)S(1)} all-reduce(f32[64]{0:T(128)S(1)} %get-tuple-element.165), channel_id=2, replica_groups=mesh['parts'=2,'seq'=4,'tok'=2,'head'=2] {'seq'}, use_global_device_ids=true, to_apply=%add | all-reduce | flops 64 | bytes 512
  30.4 1.0 add_select_fusion
  31.5 73.4 %while.14 = (s32[]{:T(128)}, f32[16,512,64]{1,2,0:T(8,128)}, f32[16,512]{1,0:T(8,128)S(1)}, f32[16,4,512]{2,1,0:T(4,128)S(1)}, f32[512,512]{1,0:T(8,128)}, /*ind...) while((s32[]{:T(128)}, f32[16,512,64]{1,2,0:T(8,128)}, ...), condition=%wide.region_3.4_spmd.clone.clone, body=%wide.region_2.3_spmd.clone.clone.sunk | while | flops 38273032 | bytes 5538319 | solution.py:65
  33.4 2.7 %fusion.68 = f32[16,512,64]{1,2,0:T(8,128)} fusion(f32[16,512,64]{1,2,0:T(8,128)} %get-tuple-element.244, s32[]{:T(128)S(6)} %copy.59, f32[512,512]{1,0:T(8,128)} %get-tuple-element.262, s32[512,512]{1,0:T(8,128)S(1)} %reshape.207, f32[512]{0:T(512)S(1)} %bitcast.97, f32[512]{0:T(512)S(1)} %bitcast.95, f32[512]{0:T(512)S(1)} %bitcast.96, ...), kind=kOutput, calls=%fused_computation.3.clone.1 | convolution fusion | flops 38273024 | bytes 2371592 | tf_op jit(solution)/shard_map/while/body/eval_jaxpr/dot_general | solution.py:63
  38.0 2.7 %fusion.68 = f32[16,512,64]{1,2,0:T(8,128)} fusion(f32[16,512,64]{1,2,0:T(8,128)} %get-tuple-element.244, s32[]{:T(128)S(6)} %copy.59, f32[512,512]{1,0:T(8,128)} %get-tuple-element.262, s32[512,512]{1,0:T(8,128)S(1)} %reshape.207, f32[512]{0:T(512)S(1)} %bitcast.97, f32[512]{0:T(512)S(1)} %bitcast.95, f32[512]{0:T(512)S(1)} %bitcast.96, ...), kind=kOutput, calls=%fused_computation.3.clone.1 | convolution fusion | flops 38273024 | bytes 2371592 | tf_op jit(solution)/shard_map/while/body/eval_jaxpr/dot_general | solution.py:63
  42.7 2.7 %fusion.68 = f32[16,512,64]{1,2,0:T(8,128)} fusion(f32[16,512,64]{1,2,0:T(8,128)} %get-tuple-element.244, s32[]{:T(128)S(6)} %copy.59, f32[512,512]{1,0:T(8,128)} %get-tuple-element.262, s32[512,512]{1,0:T(8,128)S(1)} %reshape.207, f32[512]{0:T(512)S(1)} %bitcast.97, f32[512]{0:T(512)S(1)} %bitcast.95, f32[512]{0:T(512)S(1)} %bitcast.96, ...), kind=kOutput, calls=%fused_computation.3.clone.1 | convolution fusion | flops 38273024 | bytes 2371592 | tf_op jit(solution)/shard_map/while/body/eval_jaxpr/dot_general | solution.py:63
  47.2 2.7 %fusion.68 = f32[16,512,64]{1,2,0:T(8,128)} fusion(f32[16,512,64]{1,2,0:T(8,128)} %get-tuple-element.244, s32[]{:T(128)S(6)} %copy.59, f32[512,512]{1,0:T(8,128)} %get-tuple-element.262, s32[512,512]{1,0:T(8,128)S(1)} %reshape.207, f32[512]{0:T(512)S(1)} %bitcast.97, f32[512]{0:T(512)S(1)} %bitcast.95, f32[512]{0:T(512)S(1)} %bitcast.96, ...), kind=kOutput, calls=%fused_computation.3.clone.1 | convolution fusion | flops 38273024 | bytes 2371592 | tf_op jit(solution)/shard_map/while/body/eval_jaxpr/dot_general | solution.py:63
  51.8 2.7 %fusion.68 = f32[16,512,64]{1,2,0:T(8,128)} fusion(f32[16,512,64]{1,2,0:T(8,128)} %get-tuple-element.244, s32[]{:T(128)S(6)} %copy.59, f32[512,512]{1,0:T(8,128)} %get-tuple-element.262, s32[512,512]{1,0:T(8,128)S(1)} %reshape.207, f32[512]{0:T(512)S(1)} %bitcast.97, f32[512]{0:T(512)S(1)} %bitcast.95, f32[512]{0:T(512)S(1)} %bitcast.96, ...), kind=kOutput, calls=%fused_computation.3.clone.1 | convolution fusion | flops 38273024 | bytes 2371592 | tf_op jit(solution)/shard_map/while/body/eval_jaxpr/dot_general | solution.py:63
  56.4 2.7 %fusion.68 = f32[16,512,64]{1,2,0:T(8,128)} fusion(f32[16,512,64]{1,2,0:T(8,128)} %get-tuple-element.244, s32[]{:T(128)S(6)} %copy.59, f32[512,512]{1,0:T(8,128)} %get-tuple-element.262, s32[512,512]{1,0:T(8,128)S(1)} %reshape.207, f32[512]{0:T(512)S(1)} %bitcast.97, f32[512]{0:T(512)S(1)} %bitcast.95, f32[512]{0:T(512)S(1)} %bitcast.96, ...), kind=kOutput, calls=%fused_computation.3.clone.1 | convolution fusion | flops 38273024 | bytes 2371592 | tf_op jit(solution)/shard_map/while/body/eval_jaxpr/dot_general | solution.py:63
  61.0 2.7 %fusion.68 = f32[16,512,64]{1,2,0:T(8,128)} fusion(f32[16,512,64]{1,2,0:T(8,128)} %get-tuple-element.244, s32[]{:T(128)S(6)} %copy.59, f32[512,512]{1,0:T(8,128)} %get-tuple-element.262, s32[512,512]{1,0:T(8,128)S(1)} %reshape.207, f32[512]{0:T(512)S(1)} %bitcast.97, f32[512]{0:T(512)S(1)} %bitcast.95, f32[512]{0:T(512)S(1)} %bitcast.96, ...), kind=kOutput, calls=%fused_computation.3.clone.1 | convolution fusion | flops 38273024 | bytes 2371592 | tf_op jit(solution)/shard_map/while/body/eval_jaxpr/dot_general | solution.py:63
  65.6 2.7 %fusion.68 = f32[16,512,64]{1,2,0:T(8,128)} fusion(f32[16,512,64]{1,2,0:T(8,128)} %get-tuple-element.244, s32[]{:T(128)S(6)} %copy.59, f32[512,512]{1,0:T(8,128)} %get-tuple-element.262, s32[512,512]{1,0:T(8,128)S(1)} %reshape.207, f32[512]{0:T(512)S(1)} %bitcast.97, f32[512]{0:T(512)S(1)} %bitcast.95, f32[512]{0:T(512)S(1)} %bitcast.96, ...), kind=kOutput, calls=%fused_computation.3.clone.1 | convolution fusion | flops 38273024 | bytes 2371592 | tf_op jit(solution)/shard_map/while/body/eval_jaxpr/dot_general | solution.py:63
  70.2 2.7 %fusion.68 = f32[16,512,64]{1,2,0:T(8,128)} fusion(f32[16,512,64]{1,2,0:T(8,128)} %get-tuple-element.244, s32[]{:T(128)S(6)} %copy.59, f32[512,512]{1,0:T(8,128)} %get-tuple-element.262, s32[512,512]{1,0:T(8,128)S(1)} %reshape.207, f32[512]{0:T(512)S(1)} %bitcast.97, f32[512]{0:T(512)S(1)} %bitcast.95, f32[512]{0:T(512)S(1)} %bitcast.96, ...), kind=kOutput, calls=%fused_computation.3.clone.1 | convolution fusion | flops 38273024 | bytes 2371592 | tf_op jit(solution)/shard_map/while/body/eval_jaxpr/dot_general | solution.py:63
  74.7 2.7 %fusion.68 = f32[16,512,64]{1,2,0:T(8,128)} fusion(f32[16,512,64]{1,2,0:T(8,128)} %get-tuple-element.244, s32[]{:T(128)S(6)} %copy.59, f32[512,512]{1,0:T(8,128)} %get-tuple-element.262, s32[512,512]{1,0:T(8,128)S(1)} %reshape.207, f32[512]{0:T(512)S(1)} %bitcast.97, f32[512]{0:T(512)S(1)} %bitcast.95, f32[512]{0:T(512)S(1)} %bitcast.96, ...), kind=kOutput, calls=%fused_computation.3.clone.1 | convolution fusion | flops 38273024 | bytes 2371592 | tf_op jit(solution)/shard_map/while/body/eval_jaxpr/dot_general | solution.py:63
  79.3 2.7 %fusion.68 = f32[16,512,64]{1,2,0:T(8,128)} fusion(f32[16,512,64]{1,2,0:T(8,128)} %get-tuple-element.244, s32[]{:T(128)S(6)} %copy.59, f32[512,512]{1,0:T(8,128)} %get-tuple-element.262, s32[512,512]{1,0:T(8,128)S(1)} %reshape.207, f32[512]{0:T(512)S(1)} %bitcast.97, f32[512]{0:T(512)S(1)} %bitcast.95, f32[512]{0:T(512)S(1)} %bitcast.96, ...), kind=kOutput, calls=%fused_computation.3.clone.1 | convolution fusion | flops 38273024 | bytes 2371592 | tf_op jit(solution)/shard_map/while/body/eval_jaxpr/dot_general | solution.py:63
  83.9 2.7 %fusion.68 = f32[16,512,64]{1,2,0:T(8,128)} fusion(f32[16,512,64]{1,2,0:T(8,128)} %get-tuple-element.244, s32[]{:T(128)S(6)} %copy.59, f32[512,512]{1,0:T(8,128)} %get-tuple-element.262, s32[512,512]{1,0:T(8,128)S(1)} %reshape.207, f32[512]{0:T(512)S(1)} %bitcast.97, f32[512]{0:T(512)S(1)} %bitcast.95, f32[512]{0:T(512)S(1)} %bitcast.96, ...), kind=kOutput, calls=%fused_computation.3.clone.1 | convolution fusion | flops 38273024 | bytes 2371592 | tf_op jit(solution)/shard_map/while/body/eval_jaxpr/dot_general | solution.py:63
  88.5 2.7 %fusion.68 = f32[16,512,64]{1,2,0:T(8,128)} fusion(f32[16,512,64]{1,2,0:T(8,128)} %get-tuple-element.244, s32[]{:T(128)S(6)} %copy.59, f32[512,512]{1,0:T(8,128)} %get-tuple-element.262, s32[512,512]{1,0:T(8,128)S(1)} %reshape.207, f32[512]{0:T(512)S(1)} %bitcast.97, f32[512]{0:T(512)S(1)} %bitcast.95, f32[512]{0:T(512)S(1)} %bitcast.96, ...), kind=kOutput, calls=%fused_computation.3.clone.1 | convolution fusion | flops 38273024 | bytes 2371592 | tf_op jit(solution)/shard_map/while/body/eval_jaxpr/dot_general | solution.py:63
  93.0 2.7 %fusion.68 = f32[16,512,64]{1,2,0:T(8,128)} fusion(f32[16,512,64]{1,2,0:T(8,128)} %get-tuple-element.244, s32[]{:T(128)S(6)} %copy.59, f32[512,512]{1,0:T(8,128)} %get-tuple-element.262, s32[512,512]{1,0:T(8,128)S(1)} %reshape.207, f32[512]{0:T(512)S(1)} %bitcast.97, f32[512]{0:T(512)S(1)} %bitcast.95, f32[512]{0:T(512)S(1)} %bitcast.96, ...), kind=kOutput, calls=%fused_computation.3.clone.1 | convolution fusion | flops 38273024 | bytes 2371592 | tf_op jit(solution)/shard_map/while/body/eval_jaxpr/dot_general | solution.py:63
  97.6 2.7 %fusion.68 = f32[16,512,64]{1,2,0:T(8,128)} fusion(f32[16,512,64]{1,2,0:T(8,128)} %get-tuple-element.244, s32[]{:T(128)S(6)} %copy.59, f32[512,512]{1,0:T(8,128)} %get-tuple-element.262, s32[512,512]{1,0:T(8,128)S(1)} %reshape.207, f32[512]{0:T(512)S(1)} %bitcast.97, f32[512]{0:T(512)S(1)} %bitcast.95, f32[512]{0:T(512)S(1)} %bitcast.96, ...), kind=kOutput, calls=%fused_computation.3.clone.1 | convolution fusion | flops 38273024 | bytes 2371592 | tf_op jit(solution)/shard_map/while/body/eval_jaxpr/dot_general | solution.py:63
  102.2 2.7 %fusion.68 = f32[16,512,64]{1,2,0:T(8,128)} fusion(f32[16,512,64]{1,2,0:T(8,128)} %get-tuple-element.244, s32[]{:T(128)S(6)} %copy.59, f32[512,512]{1,0:T(8,128)} %get-tuple-element.262, s32[512,512]{1,0:T(8,128)S(1)} %reshape.207, f32[512]{0:T(512)S(1)} %bitcast.97, f32[512]{0:T(512)S(1)} %bitcast.95, f32[512]{0:T(512)S(1)} %bitcast.96, ...), kind=kOutput, calls=%fused_computation.3.clone.1 | convolution fusion | flops 38273024 | bytes 2371592 | tf_op jit(solution)/shard_map/while/body/eval_jaxpr/dot_general | solution.py:63
  104.9 1.3 %fusion.57 = (f32[1,16,512]{2,0,1:T(1,128)S(1)}, f32[1,16,512]{2,0,1:T(1,128)S(1)}, f32[1,16,512]{2,0,1:T(1,128)S(1)}) fusion(f32[12,16,512]{2,0,1:T(8,128)} %copy-done.4), kind=kLoop, calls=%fused_computation.88 | loop fusion | bytes 196608 | tf_op jit(solution)/shard_map/slice | solution.py:108
  106.5 6.6 %fusion.32 = f32[2,16,128,64]{2,0,3,1:T(2,128)S(1)} fusion(f32[4,16,128,64]{2,3,1,0:T(8,128)} %bitcast.90, f32[4,16]{0,1:T(8,128)S(1)} %copy.30, f32[4,2]{0,1:T(2,128)S(1)} %compare_convert_fusion), kind=kOutput, calls=%fused_computation.40 | convolution fusion | flops 12583040 | bytes 3146016 | tf_op jit(solution)/shard_map/mh,mj,mhnp->jhnp/dot_general | solution.py:155
  113.1 1.1 fusion.56
  114.2 1.0 fusion.40
  115.2 1.0 fusion.42
  116.2 1.7 %multiply_reduce_fusion = (f32[16,512]{1,0:T(8,128)S(1)}, f32[16,512,64]{1,2,0:T(8,128)S(1)}) fusion(f32[16,512,64]{1,2,0:T(8,128)S(1)} %copy-done.3, f32[16,64,512]{2,1,0:T(8,128)S(1)} %fusion.40, f32[16,512]{1,0:T(8,128)S(1)} %get-tuple-element.169, f32[16,64,512]{2,1,0:T(8,128)S(1)} %fusion.42, f32[16,512]{1,0:T(8,128)S(1)} %get-tuple-element.170, ...), kind=kOutput, calls=%fused_computation.39 | convolution fusion | flops 810147840 | bytes 9207812 | tf_op jit(solution)/shard_map/tn,hnp->htp/dot_general | solution.py:107
  118.4 1.3 %copy.32 = bf16[512,1024]{1,0:T(8,128)(2,1)} copy(bf16[512,1024]{0,1:T(8,128)(2,1)S(1)} %bitcast.88) | data formatting | bytes 2097152 | tf_op jit(solution)/shard_map/convert_element_type | solution.py:115
  (133 shorter events, 24.0 us)
Async XLA Ops:
  6.5 8.7 %copy-start = (bf16[512,128]{1,0:T(8,128)(2,1)S(1)}, bf16[512,128]{1,0:T(8,128)(2,1)}, u32[]{:S(2)}) copy-start(bf16[512,128]{1,0:T(8,128)(2,1)} %param.14) | copy-start | bytes 393220
  6.5 7.1 %copy-start.5 = (bf16[512,128]{1,0:T(8,128)(2,1)S(1)}, bf16[512,128]{1,0:T(8,128)(2,1)}, u32[]{:S(2)}) copy-start(bf16[512,128]{1,0:T(8,128)(2,1)} %param.13) | copy-start | bytes 393220
  6.5 7.6 %copy-start.6 = (s32[12,16,512]{2,1,0:T(8,128)S(1)}, s32[12,16,512]{2,1,0:T(8,128)}, u32[]{:S(2)}) copy-start(s32[12,16,512]{2,1,0:T(8,128)} %param.16) | copy-start | bytes 1179652
  6.5 100.0 %all-gather.4.cloned.1.call-start = ((), (), s32[]{:S(2)}) async-start(), calls=%async_computation | async-start | bytes 2621440 | tf_op jit(solution)/shard_map/all_gather | solution.py:151
  9.0 8.7 %collective-permute-start.1 = (f32[16]{0:T(128)S(1)}, f32[16]{0:T(128)S(1)}, u32[]{:S(2)}, u32[]{:S(2)}) collective-permute-start(f32[16]{0:T(128)S(1)} %slice_reduce_fusion.1), channel_id=1, source_target_pairs={{0,2},{2,0},{1,3},{3,1},{4,6},{6,4},{5,7},{7,5},{8,10},{10,8},{9,1... | collective-permute-start | bytes 200 | tf_op jit(solution)/shard_map/ppermute | solution.py:19
  13.6 2.9 %copy-start.8 = (u32[32]{0:T(128)S(1)}, u32[32]{0:T(128)}, u32[]{:S(2)}) copy-start(u32[32]{0:T(128)} %constant.124) | copy-start | bytes 388
  14.1 16.3 %collective-permute-start = (f32[16,128,64]{1,2,0:T(8,128)S(1)}, f32[16,128,64]{1,2,0:T(8,128)S(1)}, u32[]{:S(2)}, u32[]{:S(2)}) collective-permute-start(f32[16,128,64]{1,2,0:T(8,128)S(1)} %convolution_bitcast_fusion.1), channel_id=1, source_target_pairs={{0,2},{2,0},{1,3},{3,1},{4,6},{6,4},{5,7},{7,5},{8,10},{10,8},{9,1... | collective-permute-start | bytes 1572872 | tf_op jit(solution)/shard_map/ppermute | solution.py:19
  14.5 0.8 copy-start.4
  30.4 1.1 copy-start.1
  31.5 74.7 %copy-start.7 = (f32[1024]{0:T(1024)S(1)}, f32[1024]{0:T(1024)}, u32[]{:S(2)}) copy-start(f32[1024]{0:T(1024)} %param.17) | copy-start | bytes 12292
  114.2 2.0 %copy-start.2 = (f32[16,128,64]{1,2,0:T(8,128)S(1)}, f32[16,128,64]{1,2,0:T(8,128)}, u32[]{:S(2)}) copy-start(f32[16,128,64]{1,2,0:T(8,128)} %copy-done.1) | copy-start | bytes 1572868
  114.2 2.0 %copy-start.3 = (f32[16,512,64]{1,2,0:T(8,128)S(1)}, f32[16,512,64]{1,2,0:T(8,128)}, u32[]{:S(2)}) copy-start(f32[16,512,64]{1,2,0:T(8,128)} %get-tuple-element.88) | copy-start | bytes 6291460
Sparse Core Ops, SparseCore 0:
  31.6 43.8 all-gather.3
where the time goes:
time: 127 us
  matrix products  54.7 us (43%)
  local copies, waits for them, and re-layouts  28.2 us (22%)
  between operations  14.2 us (11%)
  blocking collectives  12.4 us (10%)
  loops' own time  9.64 us (8%)
  other arithmetic  4.24 us (3%)
  starting transfers between devices  3.12 us (2%)
    dot_general x16, matrix products, one_head(): return jnp.dot(mixing, columns, preferred_element_type=jnp.float32)  42.7 us
    unnamed x1, blocking collectives  12.4 us
    dynamic_slice x32, local copies, waits for them, and re-layouts, near_terms(): lax.map(one_head, (cumulative, head_weights, jnp.arange(head_count, dtype...  9.67 us
    another operation x1, loops' own time, near_terms(): lax.map(one_head, (cumulative, head_weights, jnp.arange(head_count, dtype...  9.64 us
    reshape x16, local copies, waits for them, and re-layouts, near_terms(): levels_full = jnp.broadcast_to(levels[:, None, :, None], (block_rows // B...  7.83 us
    dot_general x1, matrix products, local(): jnp.einsum('mh,mj,mhnp->jhnp', coefficient, onehot, shard_piece, precisio...  6.57 us
    dot_general x3, matrix products, finish(): jnp.einsum('tn,hnp->htp', queries, far_levels[slot], precision=highest)  3.71 us
    broadcast_in_dim x16, local copies, waits for them, and re-layouts, near_terms(): jnp.broadcast_to(levels[:, None, :, None], (block_rows // BUCKET, BUCKET,...  3.19 us
  transfers between devices with their start and end apart: 3, of which 0 were waited for; matrix products, arithmetic and copies ran while one was open for 55% of the time, Pallas kernels for 0%

commit v1 on v0

v1 whole, which is shorter than its diff:
```python
import functools

import jax
import jax.numpy as jnp
from jax import lax
from jax.experimental import pallas as pl
from jax.experimental.pallas import tpu as pltpu
from jax.sharding import PartitionSpec as P

BUCKET = 64
F32 = jnp.float32
BF16 = jnp.bfloat16
MESH = pl.DeviceIdType.MESH
EXTRA = 8


def mm(a, b):
    return jnp.dot(a, b, preferred_element_type=F32)


def tmm(a, b):
    return lax.dot_general(a, b, (((0,), (0,)), ((), ())), preferred_element_type=F32)


def kernel(
    dims, v_ref, k_ref, q_ref, codes_ref, w_ref, g_ref, o_ref,
    acc, items, sel, scores, own_scores, q_twice, pref, agg, from_tok, from_seq, chain,
    tok_send, tok_recv, seq_send, seq_recv,
):
    tok_bits, seq_bits, head_size, chunk = dims
    heads, tokens = codes_ref.shape
    columns = v_ref.shape[1]
    states = k_ref.shape[1]
    chunks = columns // chunk
    near_levels = (tokens // BUCKET).bit_length() - 1
    per_group = 128 // (2 * heads)
    tok = lax.axis_index("tok")
    seq = lax.axis_index("seq")
    seq_count = 2**seq_bits
    has_next = seq + 1 < seq_count
    has_prev = seq > 0

    barrier = pltpu.get_barrier_semaphore()
    for bit in range(tok_bits):
        pl.semaphore_signal(
            barrier, inc=1, device_id={"tok": tok ^ (1 << bit)}, device_id_type=MESH
        )

    @pl.when(has_next)
    def _():
        pl.semaphore_signal(barrier, inc=1, device_id={"seq": seq + 1}, device_id_type=MESH)

    @pl.when(has_prev)
    def _():
        pl.semaphore_signal(barrier, inc=1, device_id={"seq": seq - 1}, device_id_type=MESH)

    def tok_copy(bit, c):
        return pltpu.make_async_remote_copy(
            src_ref=agg.at[bit, c],
            dst_ref=from_tok.at[bit, c],
            send_sem=tok_send.at[bit, c],
            recv_sem=tok_recv.at[bit, c],
            device_id={"tok": tok ^ (1 << bit)},
            device_id_type=MESH,
        )

    def seq_copy(source, slot, c):
        return pltpu.make_async_remote_copy(
            src_ref=source,
            dst_ref=from_seq.at[slot, c],
            send_sem=seq_send.at[slot, c],
            recv_sem=seq_recv.at[slot, c],
            device_id={"seq": lax.rem(seq + 1, seq_count)},
            device_id_type=MESH,
        )

    def cols(c):
        return slice(c * chunk, (c + 1) * chunk)

    lane = lax.broadcasted_iota(jnp.int32, (heads, tokens), 1)
    run_total = codes_ref[...]
    prefix = run_total
    before, after = {}, {}
    size = 1
    while True:
        if size >= BUCKET:
            before[size] = prefix.astype(F32) * (-1.0 / 65536.0)
            after[size] = (run_total - prefix).astype(F32) * (-1.0 / 65536.0)
        if size == tokens:
            break
        upper = (lane & size) != 0
        lower_total = pltpu.roll(run_total, size, 1)
        upper_total = pltpu.roll(run_total, tokens - size, 1)
        prefix = prefix + jnp.where(upper, lower_total, 0)
        run_total = run_total + jnp.where(upper, lower_total, upper_total)
        size *= 2
    block_total = run_total.astype(F32) * (-1.0 / 65536.0)

    row = lax.broadcasted_iota(jnp.int32, (128, columns), 0)
    column_head = lax.broadcasted_iota(jnp.int32, (128, columns), 1) // head_size
    for i in range(per_group):
        wanted = (row // (2 * heads) == i) & (row % heads == column_head)
        sel[i] = jnp.where(wanted, 1.0, 0.0).astype(BF16)
    total_row = jnp.sum(
        jnp.where(
            lax.broadcasted_iota(jnp.int32, (heads, columns), 0)
            == lax.broadcasted_iota(jnp.int32, (heads, columns), 1) // head_size,
            block_total[:, :1],
            0.0,
        ),
        axis=0,
        keepdims=True,
    )

    def put_items(group, entries):
        halves = []
        for entry in entries:
            high = entry.astype(BF16).astype(F32)
            halves += [high, entry - high]
        short = per_group - len(entries)
        if short:
            halves.append(jnp.zeros((2 * heads * short, tokens), F32))
        items[group] = jnp.transpose(jnp.concatenate(halves, axis=0)).astype(BF16)

    def spread(index, c, start=0, stop=None):
        group, i = index // per_group, index % per_group
        stop = tokens if stop is None else stop
        return mm(items[group, start:stop, :], sel[i, :, cols(c)])

    sizes = [tokens] + [BUCKET << i for i in range(near_levels)]
    key_entries = [jnp.exp(after[s]) for s in sizes]
    key_groups = -(-len(key_entries) // per_group)
    for g in range(key_groups):
        put_items(g, key_entries[g * per_group : (g + 1) * per_group])
    key_item = {s: i for i, s in enumerate(sizes)}

    pl.semaphore_wait(
        barrier, tok_bits + has_next.astype(jnp.int32) + has_prev.astype(jnp.int32)
    )
    for c in range(chunks):
        decayed = (v_ref[:, cols(c)].astype(F32) * spread(0, c)).astype(BF16)
        agg[0, c, :states, :] = tmm(k_ref[...], decayed)
        agg[0, c, states:, :] = jnp.broadcast_to(total_row[:, cols(c)], (EXTRA, chunk))
        if tok_bits:
            tok_copy(0, c).start()

    def lam(level):
        return w_ref[level].astype(F32) * (1.0 / 256.0)

    read_entries = [lam(0) * jnp.exp(-after[BUCKET])]
    for level in range(1, near_levels + 1):
        read_entries.append(lam(level) * jnp.exp(before[BUCKET << (level - 1)]))
    since_start = jnp.exp(before[tokens])
    for level in range(near_levels + 1, near_levels + 1 + tok_bits + seq_bits):
        read_entries.append(lam(level) * since_start)
    read_base = key_groups * per_group
    for g in range(-(-len(read_entries) // per_group)):
        put_items(key_groups + g, read_entries[g * per_group : (g + 1) * per_group])

    products = lax.dot_general(
        q_ref[...], k_ref[...], (((1,), (1,)), ((), ())), preferred_element_type=F32
    )
    scores[...] = products.astype(BF16)
    t_id = lax.broadcasted_iota(jnp.int32, (tokens, tokens), 0)
    s_id = lax.broadcasted_iota(jnp.int32, (tokens, tokens), 1)
    in_bucket = (t_id // BUCKET == s_id // BUCKET) & (t_id >= s_id)
    own_scores[...] = jnp.where(in_bucket, products, 0.0).astype(BF16)
    q_twice[:, :states] = q_ref[...]
    q_twice[:, states:] = q_ref[...]

    def near(c):
        here = v_ref[:, cols(c)].astype(F32)
        by_bucket = (here * spread(key_item[BUCKET], c)).astype(BF16)
        block = min(256, tokens)
        for start in range(0, tokens, block):
            rows = slice(start, start + block)
            acc[rows, cols(c)] = mm(own_scores[rows, rows], by_bucket[rows]) * spread(
                read_base, c, start, start + block
            )
        for level in range(1, near_levels + 1):
            half = BUCKET << (level - 1)
            for start in range(0, tokens, 2 * half):
                low = slice(start, start + half)
                high = slice(start + half, start + 2 * half)
                if half == BUCKET:
                    source = by_bucket[low]
                else:
                    source = (
                        here[low] * spread(key_item[half], c, start, start + half)
                    ).astype(BF16)
                acc[high, cols(c)] += mm(scores[high, low], source) * spread(
                    read_base + level, c, start + half, start + 2 * half
                )

    def far(level, payload, gap, c):
        state = payload[:states] * jnp.exp(gap)
        high = state.astype(BF16)
        low = (state - high.astype(F32)).astype(BF16)
        acc[:, cols(c)] += mm(q_twice[...], jnp.concatenate([high, low], axis=0)) * spread(
            read_base + level, c
        )

    trailing = [
        (seq & ((1 << (t + 1)) - 1)) == (1 << t) - 1 for t in range(seq_bits)
    ]

    def tok_step(bit, c):
        tok_copy(bit, c).wait_recv()
        upper = ((tok >> bit) & 1) == 1
        mine, theirs = agg.at[bit, c], from_tok.at[bit, c]
        my_total, their_total = mine[states:][:1], theirs[states:][:1]

        @pl.when(upper)
        def _():
            agg[bit + 1, c, :states] = jnp.exp(my_total) * theirs[:states] + mine[:states]

        @pl.when(jnp.logical_not(upper))
        def _():
            agg[bit + 1, c, :states] = jnp.exp(their_total) * mine[:states] + theirs[:states]

        agg[bit + 1, c, states:] = jnp.broadcast_to(my_total + their_total, (EXTRA, chunk))
        if bit + 1 < tok_bits:
            tok_copy(bit + 1, c).start()

    def tok_read(bit, c):
        @pl.when(((tok >> bit) & 1) == 1)
        def _():
            far(near_levels + 1 + bit, from_tok.at[bit, c], pref[c, :1], c)
            pref[c] += from_tok[bit, c, states:]

    for c in range(chunks):
        pref[c] = jnp.zeros((EXTRA, chunk), F32)
    for bit in range(max(tok_bits, 1)):
        for c in range(chunks):
            if bit == 0:
                near(c)
            if bit < tok_bits:
                tok_step(bit, c)
            if bit + 1 >= tok_bits and seq_bits:

                @pl.when(jnp.logical_and(has_next, trailing[0]))
                def _():
                    seq_copy(agg.at[tok_bits, c], 0, c).start()

    for bit in range(tok_bits):
        for c in range(chunks):
            tok_read(bit, c)

    def seq_step(slot, c):
        @pl.when(((seq >> slot) & 1) == 1)
        def _():
            seq_copy(agg.at[tok_bits, c], slot, c).wait_recv()

            @pl.when(jnp.logical_and(has_next, ((seq + 1) >> slot) == (seq >> slot)))
            def _():
                seq_copy(from_seq.at[slot, c], slot, c).start()

            if slot + 1 < seq_bits:

                @pl.when(jnp.logical_and(has_next, trailing[slot + 1]))
                def _():
                    total = agg[tok_bits, c, states:][:1]
                    state = agg[tok_bits, c, :states]
                    for lower in range(slot + 1):
                        state = state + jnp.exp(total) * from_seq[lower, c, :states]
                        total = total + from_seq[lower, c, states:][:1]
                    chain[c, :states] = state
                    chain[c, states:] = jnp.broadcast_to(total, (EXTRA, chunk))
                    seq_copy(chain.at[c], slot + 1, c).start()

            far(near_levels + 1 + tok_bits + slot, from_seq.at[slot, c], pref[c, :1], c)
            pref[c] += from_seq[slot, c, states:]

    group_row = lax.broadcasted_iota(jnp.int32, (chunk, chunk), 0) // head_size
    group_col = lax.broadcasted_iota(jnp.int32, (chunk, chunk), 1) // head_size
    same_head = jnp.where(group_row == group_col, 1.0, 0.0).astype(BF16)

    def norm(c):
        y = acc[:, cols(c)]
        mean = mm((y * y).astype(BF16), same_head) * (1.0 / head_size)
        o_ref[:, cols(c)] = (y * lax.rsqrt(mean + 1e-5) * g_ref[:, cols(c)]).astype(o_ref.dtype)

    for slot in range(seq_bits):
        for c in range(chunks):
            seq_step(slot, c)
            if slot == seq_bits - 1:
                norm(c)
    if not seq_bits:
        for c in range(chunks):
            norm(c)

    for bit in range(tok_bits):
        for c in range(chunks):
            tok_copy(bit, c).wait_send()
    for slot in range(seq_bits):
        for c in range(chunks):

            @pl.when(jnp.logical_and(has_next, (((seq + 1) >> slot) & 1) == 1))
            def _():
                seq_copy(from_seq.at[slot, c], slot, c).wait_send()


def local(values, key_rows, query_rows, decay_codes, weight_codes, norm_gain):
    heads, tokens = decay_codes.shape
    columns = values.shape[1]
    states = key_rows.shape[1]
    head_size = columns // heads
    chunk = min(256, columns)
    chunks = columns // chunk
    tok_bits = lax.axis_size("tok").bit_length() - 1
    seq_bits = lax.axis_size("seq").bit_length() - 1
    near_levels = (tokens // BUCKET).bit_length() - 1
    per_group = 128 // (2 * heads)
    groups = -(-(near_levels + 1) // per_group) - (
        -(near_levels + 1 + tok_bits + seq_bits) // per_group
    )
    parcel = (chunks, states + EXTRA, chunk)
    vmem = pl.BlockSpec(memory_space=pltpu.VMEM)
    return pl.pallas_call(
        functools.partial(kernel, (tok_bits, seq_bits, head_size, chunk)),
        out_shape=jax.ShapeDtypeStruct((tokens, columns), values.dtype),
        in_specs=[vmem] * 6,
        out_specs=vmem,
        scratch_shapes=[
            pltpu.VMEM((tokens, columns), F32),
            pltpu.VMEM((groups, tokens, 128), BF16),
            pltpu.VMEM((per_group, 128, columns), BF16),
            pltpu.VMEM((tokens, tokens), BF16),
            pltpu.VMEM((tokens, tokens), BF16),
            pltpu.VMEM((tokens, 2 * states), BF16),
            pltpu.VMEM((chunks, EXTRA, chunk), F32),
            pltpu.VMEM((tok_bits + 1,) + parcel, F32),
            pltpu.VMEM((max(tok_bits, 1),) + parcel, F32),
            pltpu.VMEM((max(seq_bits, 1),) + parcel, F32),
            pltpu.VMEM(parcel, F32),
            pltpu.SemaphoreType.DMA((max(tok_bits, 1), chunks)),
            pltpu.SemaphoreType.DMA((max(tok_bits, 1), chunks)),
            pltpu.SemaphoreType.DMA((max(seq_bits, 1), chunks)),
            pltpu.SemaphoreType.DMA((max(seq_bits, 1), chunks)),
        ],
        compiler_params=pltpu.CompilerParams(collective_id=0, has_side_effects=True),
    )(values, key_rows, query_rows, decay_codes, weight_codes, norm_gain.reshape(1, columns))


def solution(mesh):
    return jax.shard_map(
        local,
        mesh=mesh,
        in_specs=(
            P(("parts", "seq", "tok"), "head"),
            P(("parts", "seq", "tok"), None),
            P(("parts", "seq", "tok"), None),
            P("head", ("parts", "seq", "tok")),
            P(None, "head", ("parts", "seq", "tok")),
            P("head"),
        ),
        out_specs=P(("parts", "seq", "tok"), "head"),
        check_vma=False,
    )
```

time: 127 us -> 38.1 us (0.30)
  the two profiles are of different devices: /device:TPU:0 before, /device:TPU:24 now
where the time goes in v1:
time: 38.1 us; the launch traced here: 37.9 us
  Pallas kernels  35.6 us (93%)
  local copies, waits for them, and re-layouts  2.26 us (6%)
    pallas_call x1, Pallas kernels, local(): pl.pallas_call(functools.partial(kernel, (tok_bits, seq_bits, head_size,...  35.6 us
    unnamed x1, local copies, waits for them, and re-layouts  2.26 us

profile of v1, /device:TPU:24, one launch (start us, length us, event | category | flops | bytes accessed | tf_op | source)
XLA Modules:
  0.0 37.9 jit_solution(12102423145261480250)
XLA Ops:
  0.0 35.6 %shard_map.64 = bf16[512,1024]{1,0:T(8,128)(2,1)} custom-call(bf16[512,1024]{1,0:T(8,128)(2,1)} %v_ref.1, bf16[512,128]{1,0:T(8,128)(2,1)} %k_ref.1, bf16[512,128]{1,0:T(8,128)(2,1)} %q_ref.1, s32[16,512]{1,0:T(8,128)} %codes_ref.1, s32[12,16,512]{2,1,0:T(8,128)} %w_ref.1, f32[1,1024]{1,0:T(1,128)} %bitcast.1), custom_call_target="tpu_custom_call" | custom-call | tf_op jit(solution)/shard_map/pallas_call | solution.py:319
  35.6 2.3 %copy.8 = bf16[512,1024]{1,0:T(8,128)(2,1)} copy(bf16[512,1024]{1,0:T(8,128)(2,1)} %shard_map.64) | data formatting | bytes 2097152

commit v2 on v1

v2 whole, which is shorter than its diff:
```python
import functools

import jax
import jax.numpy as jnp
from jax import lax
from jax.experimental import pallas as pl
from jax.experimental.pallas import tpu as pltpu
from jax.sharding import PartitionSpec as P

BUCKET = 64
F32 = jnp.float32
BF16 = jnp.bfloat16
MESH = pl.DeviceIdType.MESH
LANES = 128


def mm(a, b):
    return jnp.dot(a, b, preferred_element_type=F32)


def tmm(a, b):
    return lax.dot_general(a, b, (((0,), (0,)), ((), ())), preferred_element_type=F32)


def kernel(
    dims, v_hbm, k_hbm, q_hbm, codes_hbm, w_hbm, o_ref,
    v_ref, k_ref, q_ref, codes_ref, w_ref, load_sem,
    acc, items, sel, scores, own_scores, q_twice, agg, from_tok, from_seq, chain,
    pref, agg_total, tok_total, seq_total, chain_total,
    tok_send, tok_recv, seq_send, seq_recv, swap_send, swap_recv,
):
    tok_bits, seq_bits, head_size, chunk = dims
    heads, tokens = codes_ref.shape
    columns = v_ref.shape[1]
    states = k_ref.shape[1]
    chunks = columns // chunk
    near_levels = (tokens // BUCKET).bit_length() - 1
    per_group = 128 // (2 * heads)
    tok = lax.axis_index("tok")
    seq = lax.axis_index("seq")
    seq_count = 2**seq_bits
    has_next = seq + 1 < seq_count
    has_prev = seq > 0

    def load(i):
        source, target = (
            (codes_hbm, codes_ref), (k_hbm, k_ref), (v_hbm, v_ref), (q_hbm, q_ref), (w_hbm, w_ref)
        )[i]
        return pltpu.make_async_copy(source, target, load_sem.at[i])

    for i in range(5):
        load(i).start()

    barrier = pltpu.get_barrier_semaphore()
    for bit in range(tok_bits):
        pl.semaphore_signal(
            barrier, inc=1, device_id={"tok": tok ^ (1 << bit)}, device_id_type=MESH
        )

    @pl.when(has_next)
    def _():
        pl.semaphore_signal(barrier, inc=1, device_id={"seq": seq + 1}, device_id_type=MESH)

    @pl.when(has_prev)
    def _():
        pl.semaphore_signal(barrier, inc=1, device_id={"seq": seq - 1}, device_id_type=MESH)

    half = states // 2
    mine_at = pl.multiple_of((tok & 1) * half, half)
    other_at = pl.multiple_of((1 - (tok & 1)) * half, half)
    after_me = lax.rem(seq + 1, seq_count)

    def splits(slot):
        return slot > 0 and tok_bits > 0

    def tok_copy(bit, c):
        totals = c == chunks
        return pltpu.make_async_remote_copy(
            src_ref=agg_total.at[bit] if totals else agg.at[bit, c],
            dst_ref=tok_total.at[bit] if totals else from_tok.at[bit, c],
            send_sem=tok_send.at[bit, c],
            recv_sem=tok_recv.at[bit, c],
            device_id={"tok": tok ^ (1 << bit)},
            device_id_type=MESH,
        )

    def seq_copy(source, slot, c):
        if c == chunks:
            target = seq_total.at[slot]
        else:
            target = from_seq.at[slot, c]
            if splits(slot):
                source = source.at[pl.ds(mine_at, half)]
                target = target.at[pl.ds(mine_at, half)]
        return pltpu.make_async_remote_copy(
            src_ref=source,
            dst_ref=target,
            send_sem=seq_send.at[slot, c],
            recv_sem=seq_recv.at[slot, c],
            device_id={"seq": after_me},
            device_id_type=MESH,
        )

    def swap_copy(slot, c, at):
        place = from_seq.at[slot, c, pl.ds(at, half)]
        return pltpu.make_async_remote_copy(
            src_ref=place,
            dst_ref=place,
            send_sem=swap_send.at[slot, c],
            recv_sem=swap_recv.at[slot, c],
            device_id={"tok": tok ^ 1},
            device_id_type=MESH,
        )

    pieces = chunk // LANES

    def row_of(total, c):
        return jnp.concatenate(
            [total[c * pieces + i : c * pieces + i + 1, :] for i in range(pieces)], axis=1
        )

    def cols(c):
        return slice(c * chunk, (c + 1) * chunk)

    load(0).wait()
    lane = lax.broadcasted_iota(jnp.int32, (heads, tokens), 1)
    run_total = codes_ref[...]
    prefix = run_total
    before, after = {}, {}
    size = 1
    while True:
        if size >= BUCKET:
            before[size] = prefix.astype(F32) * (-1.0 / 65536.0)
            after[size] = (run_total - prefix).astype(F32) * (-1.0 / 65536.0)
        if size == tokens:
            break
        upper = (lane & size) != 0
        lower_total = pltpu.roll(run_total, size, 1)
        upper_total = pltpu.roll(run_total, tokens - size, 1)
        prefix = prefix + jnp.where(upper, lower_total, 0)
        run_total = run_total + jnp.where(upper, lower_total, upper_total)
        size *= 2
    block_total = run_total.astype(F32) * (-1.0 / 65536.0)

    head_shift = head_size.bit_length() - 1
    item_shift = (2 * heads).bit_length() - 1

    def put_sel(i):
        row = lax.broadcasted_iota(jnp.int32, (LANES, columns), 0)
        column_head = lax.broadcasted_iota(jnp.int32, (LANES, columns), 1) >> head_shift
        wanted = ((row >> item_shift) == i) & ((row & (heads - 1)) == column_head)
        sel[i] = jnp.where(wanted, 1.0, 0.0).astype(BF16)

    put_sel(0)
    total_row = jnp.sum(
        jnp.where(
            lax.broadcasted_iota(jnp.int32, (heads, columns), 0)
            == lax.broadcasted_iota(jnp.int32, (heads, columns), 1) >> head_shift,
            block_total[:, :1],
            0.0,
        ),
        axis=0,
        keepdims=True,
    )

    def put_items(group, entries):
        halves = []
        for entry in entries:
            high = entry.astype(BF16).astype(F32)
            halves += [high, entry - high]
        short = per_group - len(entries)
        if short:
            halves.append(jnp.zeros((2 * heads * short, tokens), F32))
        items[group] = jnp.transpose(jnp.concatenate(halves, axis=0)).astype(BF16)

    def spread(index, c, start=0, stop=None):
        group, i = index // per_group, index % per_group
        stop = tokens if stop is None else stop
        return mm(items[group, start:stop, :], sel[i, :, cols(c)])

    sizes = [tokens] + [BUCKET << i for i in range(near_levels)]
    key_entries = [jnp.exp(after[s]) for s in sizes]
    key_groups = -(-len(key_entries) // per_group)
    for g in range(key_groups):
        put_items(g, key_entries[g * per_group : (g + 1) * per_group])
    key_item = {s: i for i, s in enumerate(sizes)}

    for r in range(columns // LANES):
        agg_total[0, r : r + 1] = total_row[:, r * LANES : (r + 1) * LANES]
    load(1).wait()
    load(2).wait()
    pl.semaphore_wait(
        barrier, tok_bits + has_next.astype(jnp.int32) + has_prev.astype(jnp.int32)
    )
    for c in range(chunks):
        decayed = (v_ref[:, cols(c)].astype(F32) * spread(0, c)).astype(BF16)
        agg[0, c] = tmm(k_ref[...], decayed)
        if tok_bits:
            if c == 0:
                tok_copy(0, chunks).start()
            tok_copy(0, c).start()
    for i in range(1, per_group):
        put_sel(i)

    load(3).wait()
    load(4).wait()

    def lam(level):
        return w_ref[level].astype(F32) * (1.0 / 256.0)

    read_entries = [lam(0) * jnp.exp(-after[BUCKET])]
    for level in range(1, near_levels + 1):
        read_entries.append(lam(level) * jnp.exp(before[BUCKET << (level - 1)]))
    since_start = jnp.exp(before[tokens])
    for level in range(near_levels + 1, near_levels + 1 + tok_bits + seq_bits):
        read_entries.append(lam(level) * since_start)
    read_base = key_groups * per_group
    for g in range(-(-len(read_entries) // per_group)):
        put_items(key_groups + g, read_entries[g * per_group : (g + 1) * per_group])

    products = lax.dot_general(
        q_ref[...], k_ref[...], (((1,), (1,)), ((), ())), preferred_element_type=F32
    )
    scores[...] = products.astype(BF16)
    t_id = lax.broadcasted_iota(jnp.int32, (tokens, tokens), 0)
    s_id = lax.broadcasted_iota(jnp.int32, (tokens, tokens), 1)
    bucket_shift = BUCKET.bit_length() - 1
    in_bucket = ((t_id >> bucket_shift) == (s_id >> bucket_shift)) & (t_id >= s_id)
    own_scores[...] = jnp.where(in_bucket, products, 0.0).astype(BF16)
    q_twice[:, :states] = q_ref[...]
    q_twice[:, states:] = q_ref[...]

    def near(c):
        here = v_ref[:, cols(c)].astype(F32)
        by_bucket = (here * spread(key_item[BUCKET], c)).astype(BF16)
        block = min(256, tokens)
        for start in range(0, tokens, block):
            rows = slice(start, start + block)
            acc[rows, cols(c)] = mm(own_scores[rows, rows], by_bucket[rows]) * spread(
                read_base, c, start, start + block
            )
        for level in range(1, near_levels + 1):
            run = BUCKET << (level - 1)
            for start in range(0, tokens, 2 * run):
                low = slice(start, start + run)
                high = slice(start + run, start + 2 * run)
                if run == BUCKET:
                    source = by_bucket[low]
                else:
                    source = (
                        here[low] * spread(key_item[run], c, start, start + run)
                    ).astype(BF16)
                acc[high, cols(c)] += mm(scores[high, low], source) * spread(
                    read_base + level, c, start + run, start + 2 * run
                )

    def far(level, payload, gap, c):
        state = payload[...] * jnp.exp(gap)
        high = state.astype(BF16)
        low = (state - high.astype(F32)).astype(BF16)
        acc[:, cols(c)] += mm(q_twice[...], jnp.concatenate([high, low], axis=0)) * spread(
            read_base + level, c
        )

    trailing = [
        (seq & ((1 << (t + 1)) - 1)) == (1 << t) - 1 for t in range(seq_bits)
    ]

    def tok_step(bit, c):
        tok_copy(bit, c).wait_recv()
        upper = ((tok >> bit) & 1) == 1
        mine, theirs = agg.at[bit, c], from_tok.at[bit, c]
        my_total, their_total = row_of(agg_total.at[bit], c), row_of(tok_total.at[bit], c)

        @pl.when(upper)
        def _():
            agg[bit + 1, c] = jnp.exp(my_total) * theirs[...] + mine[...]

        @pl.when(jnp.logical_not(upper))
        def _():
            agg[bit + 1, c] = jnp.exp(their_total) * mine[...] + theirs[...]

        if bit + 1 < tok_bits:
            tok_copy(bit + 1, c).start()

    def tok_totals(bit):
        tok_copy(bit, chunks).wait_recv()
        upper = ((tok >> bit) & 1) == 1
        agg_total[bit + 1] = agg_total[bit] + tok_total[bit]
        pref[bit + 1] = pref[bit] + jnp.where(upper, tok_total[bit], 0.0)
        if bit + 1 < tok_bits:
            tok_copy(bit + 1, chunks).start()

    def tok_read(bit, c):
        @pl.when(((tok >> bit) & 1) == 1)
        def _():
            far(near_levels + 1 + bit, from_tok.at[bit, c], row_of(pref.at[bit], c), c)

    sends_own = jnp.logical_and(has_next, trailing[0]) if seq_bits else None
    pref[0] = jnp.zeros(pref.shape[1:], F32)
    for bit in range(max(tok_bits, 1)):
        for c in range(chunks):
            if bit == 0:
                near(c)
            if bit < tok_bits:
                if c == 0:
                    tok_totals(bit)
                tok_step(bit, c)
            if bit + 1 >= tok_bits and seq_bits:

                @pl.when(sends_own)
                def _():
                    if c == 0:
                        seq_copy(agg_total.at[tok_bits], 0, chunks).start()
                    seq_copy(agg.at[tok_bits, c], 0, c).start()

            if bit < tok_bits:
                tok_read(bit, c)

    def held(slot):
        return ((seq >> slot) & 1) == 1

    def forwards(slot):
        return jnp.logical_and(has_next, ((seq + 1) >> slot) == (seq >> slot))

    def chains(slot):
        return jnp.logical_and(has_next, trailing[slot])

    def seq_totals(slot):
        stage = tok_bits + slot

        @pl.when(held(slot))
        def _():
            seq_copy(agg_total.at[tok_bits], slot, chunks).wait_recv()
            pref[stage + 1] = pref[stage] + seq_total[slot]

            @pl.when(forwards(slot))
            def _():
                seq_copy(seq_total.at[slot], slot, chunks).start()

            if slot + 1 < seq_bits:

                @pl.when(chains(slot + 1))
                def _():
                    total = agg_total[tok_bits]
                    for lower in range(slot + 1):
                        total = total + seq_total[lower]
                    chain_total[...] = total
                    seq_copy(chain_total, slot + 1, chunks).start()

        @pl.when(jnp.logical_not(held(slot)))
        def _():
            pref[stage + 1] = pref[stage]

    def seq_step(slot, c):
        @pl.when(held(slot))
        def _():
            seq_copy(agg.at[tok_bits, c], slot, c).wait_recv()

            @pl.when(forwards(slot))
            def _():
                seq_copy(from_seq.at[slot, c], slot, c).start()

            if splits(slot):
                swap_copy(slot, c, mine_at).start()

            if slot + 1 < seq_bits:

                @pl.when(chains(slot + 1))
                def _():
                    rows = pl.ds(mine_at, half) if splits(slot + 1) else slice(None)
                    total = row_of(agg_total.at[tok_bits], c)
                    state = agg[tok_bits, c, rows]
                    for lower in range(slot + 1):
                        state = state + jnp.exp(total) * from_seq[lower, c, rows]
                        total = total + row_of(seq_total.at[lower], c)
                    chain[c, rows] = state
                    seq_copy(chain.at[c], slot + 1, c).start()

    def seq_read(slot, c):
        @pl.when(held(slot))
        def _():
            if splits(slot):
                swap_copy(slot, c, other_at).wait_recv()
            far(
                near_levels + 1 + tok_bits + slot,
                from_seq.at[slot, c],
                row_of(pref.at[tok_bits + slot], c),
                c,
            )

    group_row = lax.broadcasted_iota(jnp.int32, (chunk, chunk), 0) >> head_shift
    group_col = lax.broadcasted_iota(jnp.int32, (chunk, chunk), 1) >> head_shift
    same_head = jnp.where(group_row == group_col, 1.0, 0.0).astype(BF16)

    def norm(c):
        y = acc[:, cols(c)]
        mean = mm((y * y).astype(BF16), same_head) * (1.0 / head_size)
        o_ref[:, cols(c)] = y * lax.rsqrt(mean + 1e-5)

    for slot in range(seq_bits):
        behind = 1 if splits(slot) else 0
        seq_totals(slot)
        for c in range(chunks + behind):
            if c < chunks:
                seq_step(slot, c)
            if c >= behind:
                seq_read(slot, c - behind)
                if slot == seq_bits - 1:
                    norm(c - behind)
    if not seq_bits:
        for c in range(chunks):
            norm(c)

    for bit in range(tok_bits):
        for c in range(chunks + 1):
            tok_copy(bit, c).wait_send()
    for slot in range(seq_bits):

        @pl.when(jnp.logical_and(has_next, (((seq + 1) >> slot) & 1) == 1))
        def _():
            for c in range(chunks + 1):
                source = seq_total.at[slot] if c == chunks else from_seq.at[slot, c]
                seq_copy(source, slot, c).wait_send()

        if splits(slot):

            @pl.when(held(slot))
            def _():
                for c in range(chunks):
                    swap_copy(slot, c, mine_at).wait_send()


def local(values, key_rows, query_rows, decay_codes, weight_codes, norm_gain):
    heads, tokens = decay_codes.shape
    columns = values.shape[1]
    states = key_rows.shape[1]
    head_size = columns // heads
    chunk = min(256, columns)
    chunks = columns // chunk
    tok_bits = lax.axis_size("tok").bit_length() - 1
    seq_bits = lax.axis_size("seq").bit_length() - 1
    near_levels = (tokens // BUCKET).bit_length() - 1
    per_group = 128 // (2 * heads)
    groups = -(-(near_levels + 1) // per_group) - (
        -(near_levels + 1 + tok_bits + seq_bits) // per_group
    )
    parcel = (chunks, states, chunk)
    totals = (columns // LANES, LANES)
    tok_slots, seq_slots = max(tok_bits, 1), max(seq_bits, 1)
    vmem = pl.BlockSpec(memory_space=pltpu.VMEM)
    normed = pl.pallas_call(
        functools.partial(kernel, (tok_bits, seq_bits, head_size, chunk)),
        out_shape=jax.ShapeDtypeStruct((tokens, columns), F32),
        in_specs=[pl.BlockSpec(memory_space=pltpu.HBM)] * 5,
        out_specs=vmem,
        scratch_shapes=[
            *(
                pltpu.VMEM(x.shape, x.dtype)
                for x in (values, key_rows, query_rows, decay_codes, weight_codes)
            ),
            pltpu.SemaphoreType.DMA((5,)),
            pltpu.VMEM((tokens, columns), F32),
            pltpu.VMEM((groups, tokens, LANES), BF16),
            pltpu.VMEM((per_group, LANES, columns), BF16),
            pltpu.VMEM((tokens, tokens), BF16),
            pltpu.VMEM((tokens, tokens), BF16),
            pltpu.VMEM((tokens, 2 * states), BF16),
            pltpu.VMEM((tok_bits + 1,) + parcel, F32),
            pltpu.VMEM((tok_slots,) + parcel, F32),
            pltpu.VMEM((seq_slots,) + parcel, F32),
            pltpu.VMEM(parcel, F32),
            pltpu.VMEM((tok_bits + seq_bits + 1,) + totals, F32),
            pltpu.VMEM((tok_bits + 1,) + totals, F32),
            pltpu.VMEM((tok_slots,) + totals, F32),
            pltpu.VMEM((seq_slots,) + totals, F32),
            pltpu.VMEM(totals, F32),
            pltpu.SemaphoreType.DMA((tok_slots, chunks + 1)),
            pltpu.SemaphoreType.DMA((tok_slots, chunks + 1)),
            pltpu.SemaphoreType.DMA((seq_slots, chunks + 1)),
            pltpu.SemaphoreType.DMA((seq_slots, chunks + 1)),
            pltpu.SemaphoreType.DMA((seq_slots, chunks)),
            pltpu.SemaphoreType.DMA((seq_slots, chunks)),
        ],
        compiler_params=pltpu.CompilerParams(
            collective_id=0, has_side_effects=True, vmem_limit_bytes=40 * 2**20
        ),
    )(values, key_rows, query_rows, decay_codes, weight_codes)
    return (normed * norm_gain[None, :]).astype(values.dtype)


def solution(mesh):
    return jax.shard_map(
        local,
        mesh=mesh,
        in_specs=(
            P(("parts", "seq", "tok"), "head"),
            P(("parts", "seq", "tok"), None),
            P(("parts", "seq", "tok"), None),
            P("head", ("parts", "seq", "tok")),
            P(None, "head", ("parts", "seq", "tok")),
            P("head"),
        ),
        out_specs=P(("parts", "seq", "tok"), "head"),
        check_vma=False,
    )
```

time: 38.1 us -> 39.2 us (1.029)
  Pallas kernels: 35.6 us -> 32.9 us
  local copies, waits for them, and re-layouts: 2.26 us -> 4.79 us
  other arithmetic: 0 us -> 1.23 us
    pallas_call x1, Pallas kernels: 35.6 us -> 32.9 us  [local(): pl.pallas_call(functools.partial(kernel, (tok_bits, seq_bits, head_size,...]
    unnamed x1 -> x12, local copies, waits for them, and re-layouts: 2.26 us -> 4.79 us
    convert_element_type x0 -> x1, other arithmetic: none -> 1.23 us  [local(): return (normed * norm_gain[None, :]).astype(values.dtype)]
where the time goes in v2:
time: 39.2 us; the launch traced here: 38.9 us
  Pallas kernels  32.9 us (84%)
  local copies, waits for them, and re-layouts  4.79 us (12%)
  other arithmetic  1.23 us (3%)
    pallas_call x1, Pallas kernels, local(): pl.pallas_call(functools.partial(kernel, (tok_bits, seq_bits, head_size,...  32.9 us
    unnamed x12, local copies, waits for them, and re-layouts  4.79 us
    convert_element_type x1, other arithmetic, local(): return (normed * norm_gain[None, :]).astype(values.dtype)  1.23 us

profile of v2, /device:TPU:24, one launch (start us, length us, event | category | flops | bytes accessed | tf_op | source)
XLA Modules:
  0.0 38.9 jit_solution(7222129546588580566)
XLA Ops:
  0.0 0.0 copy-start
  0.0 1.2 %copy-done = bf16[512,1024]{1,0:T(8,128)(2,1)S(1)} copy-done((bf16[512,1024]{1,0:T(8,128)(2,1)S(1)}, bf16[512,1024]{1,0:T(8,128)(2,1)}, u32[]{:S(2)}) %copy-start) | copy-done | bytes 1048600
  1.2 0.0 copy-start.1
  1.2 1.0 %copy-done.1 = s32[12,16,512]{2,1,0:T(8,128)S(1)} copy-done((s32[12,16,512]{2,1,0:T(8,128)S(1)}, s32[12,16,512]{2,1,0:T(8,128)}, u32[]{:S(2)}) %copy-start.1) | copy-done | bytes 393240
  2.2 0.0 copy-start.2
  2.2 0.9 %copy-done.2 = bf16[512,128]{1,0:T(8,128)(2,1)S(1)} copy-done((bf16[512,128]{1,0:T(8,128)(2,1)S(1)}, bf16[512,128]{1,0:T(8,128)(2,1)}, u32[]{:S(2)}) %copy-start.2) | copy-done | bytes 131096
  3.1 0.0 copy-start.3
  3.1 0.9 %copy-done.3 = bf16[512,128]{1,0:T(8,128)(2,1)S(1)} copy-done((bf16[512,128]{1,0:T(8,128)(2,1)S(1)}, bf16[512,128]{1,0:T(8,128)(2,1)}, u32[]{:S(2)}) %copy-start.3) | copy-done | bytes 131096
  4.0 0.0 copy-start.4
  4.0 0.8 %copy-done.4 = s32[16,512]{1,0:T(8,128)S(1)} copy-done((s32[16,512]{1,0:T(8,128)S(1)}, s32[16,512]{1,0:T(8,128)}, u32[]{:S(2)}) %copy-start.4) | copy-done | bytes 32792
  4.8 0.0 copy-start.5
  4.8 32.9 %shard_map.64 = f32[512,1024]{1,0:T(8,128)S(1)} custom-call(bf16[512,1024]{1,0:T(8,128)(2,1)S(1)} %copy-done, bf16[512,128]{1,0:T(8,128)(2,1)S(1)} %copy-done.2, bf16[512,128]{1,0:T(8,128)(2,1)S(1)} %copy-done.3, s32[16,512]{1,0:T(8,128)S(1)} %copy-done.4, s32[12,16,512]{2,1,0:T(8,128)S(1)} %copy-done.1), custom_call_target="tpu_custom_call" | custom-call | tf_op jit(solution)/shard_map/pallas_call | solution.py:452
  37.7 0.0 copy-done.5
  37.7 1.2 %multiply_convert_fusion = bf16[512,1024]{1,0:T(8,128)(2,1)} fusion(f32[512,1024]{1,0:T(8,128)S(1)} %shard_map.64, f32[1024]{0:T(1024)S(1)} %copy-done.5), kind=kLoop, calls=%fused_computation | loop fusion | flops 1048576 | bytes 3149824 | tf_op jit(solution)/shard_map/convert_element_type | solution.py:489
Async XLA Ops:
  0.0 1.2 %copy-start = (bf16[512,1024]{1,0:T(8,128)(2,1)S(1)}, bf16[512,1024]{1,0:T(8,128)(2,1)}, u32[]{:S(2)}) copy-start(bf16[512,1024]{1,0:T(8,128)(2,1)} %v_hbm.1) | copy-start | bytes 3145732
  1.2 1.0 %copy-start.1 = (s32[12,16,512]{2,1,0:T(8,128)S(1)}, s32[12,16,512]{2,1,0:T(8,128)}, u32[]{:S(2)}) copy-start(s32[12,16,512]{2,1,0:T(8,128)} %w_hbm.1) | copy-start | bytes 1179652
  2.2 0.9 %copy-start.2 = (bf16[512,128]{1,0:T(8,128)(2,1)S(1)}, bf16[512,128]{1,0:T(8,128)(2,1)}, u32[]{:S(2)}) copy-start(bf16[512,128]{1,0:T(8,128)(2,1)} %k_hbm.1) | copy-start | bytes 393220
  3.1 0.9 %copy-start.3 = (bf16[512,128]{1,0:T(8,128)(2,1)S(1)}, bf16[512,128]{1,0:T(8,128)(2,1)}, u32[]{:S(2)}) copy-start(bf16[512,128]{1,0:T(8,128)(2,1)} %q_hbm.1) | copy-start | bytes 393220
  4.0 0.8 %copy-start.4 = (s32[16,512]{1,0:T(8,128)S(1)}, s32[16,512]{1,0:T(8,128)}, u32[]{:S(2)}) copy-start(s32[16,512]{1,0:T(8,128)} %codes_hbm.1) | copy-start | bytes 98308
  4.8 32.9 %copy-start.5 = (f32[1024]{0:T(1024)S(1)}, f32[1024]{0:T(1024)}, u32[]{:S(2)}) copy-start(f32[1024]{0:T(1024)} %param.11) | copy-start | bytes 12292

commit v3 on v2

--- a/solution.py
+++ b/solution.py
@@ -70,33 +70,39 @@
     other_at = pl.multiple_of((1 - (tok & 1)) * half, half)
     after_me = lax.rem(seq + 1, seq_count)
 
-    def splits(slot):
-        return slot > 0 and tok_bits > 0
-
-    def tok_copy(bit, c):
-        totals = c == chunks
+    def rows_of(part):
+        return pl.ds(mine_at if part == 0 else other_at, half)
+
+    def tok_copy(bit, c, part=0):
+        if c == chunks:
+            source, target = agg_total.at[bit], tok_total.at[bit]
+            slot = 2 * chunks
+        else:
+            rows = rows_of(1 - part if bit == 0 else part)
+            source, target = agg.at[bit, c, rows], from_tok.at[bit, c, rows]
+            slot = 2 * c + part
         return pltpu.make_async_remote_copy(
-            src_ref=agg_total.at[bit] if totals else agg.at[bit, c],
-            dst_ref=tok_total.at[bit] if totals else from_tok.at[bit, c],
-            send_sem=tok_send.at[bit, c],
-            recv_sem=tok_recv.at[bit, c],
+            src_ref=source,
+            dst_ref=target,
+            send_sem=tok_send.at[bit, slot],
+            recv_sem=tok_recv.at[bit, slot],
             device_id={"tok": tok ^ (1 << bit)},
             device_id_type=MESH,
         )
 
-    def seq_copy(source, slot, c):
+    def seq_copy(source, slot, c, part=0):
         if c == chunks:
             target = seq_total.at[slot]
+            place = 2 * chunks
         else:
-            target = from_seq.at[slot, c]
-            if splits(slot):
-                source = source.at[pl.ds(mine_at, half)]
-                target = target.at[pl.ds(mine_at, half)]
+            source = source.at[rows_of(part)]
+            target = from_seq.at[slot, c, rows_of(part)]
+            place = 2 * c + part
         return pltpu.make_async_remote_copy(
             src_ref=source,
             dst_ref=target,
-            send_sem=seq_send.at[slot, c],
-            recv_sem=seq_recv.at[slot, c],
+            send_sem=seq_send.at[slot, place],
+            recv_sem=seq_recv.at[slot, place],
             device_id={"seq": after_me},
             device_id_type=MESH,
         )
@@ -195,10 +201,11 @@
     for c in range(chunks):
         decayed = (v_ref[:, cols(c)].astype(F32) * spread(0, c)).astype(BF16)
         agg[0, c] = tmm(k_ref[...], decayed)
-        if tok_bits:
-            if c == 0:
-                tok_copy(0, chunks).start()
-            tok_copy(0, c).start()
+        if c == 0:
+            tok_copy(0, chunks).start()
+        tok_copy(0, c, 0).start()
+    for c in range(chunks):
+        tok_copy(0, c, 1).start()
     for i in range(1, per_group):
         put_sel(i)
 
@@ -266,22 +273,35 @@
         (seq & ((1 << (t + 1)) - 1)) == (1 << t) - 1 for t in range(seq_bits)
     ]
 
-    def tok_step(bit, c):
-        tok_copy(bit, c).wait_recv()
+    sends_own = jnp.logical_and(has_next, trailing[0]) if seq_bits else None
+
+    def tok_step(bit, c, part):
+        tok_copy(bit, c, part).wait_recv()
         upper = ((tok >> bit) & 1) == 1
-        mine, theirs = agg.at[bit, c], from_tok.at[bit, c]
+        rows = rows_of(part)
         my_total, their_total = row_of(agg_total.at[bit], c), row_of(tok_total.at[bit], c)
 
         @pl.when(upper)
         def _():
-            agg[bit + 1, c] = jnp.exp(my_total) * theirs[...] + mine[...]
+            agg[bit + 1, c, rows] = (
+                jnp.exp(my_total) * from_tok[bit, c, rows] + agg[bit, c, rows]
+            )
 
         @pl.when(jnp.logical_not(upper))
         def _():
-            agg[bit + 1, c] = jnp.exp(their_total) * mine[...] + theirs[...]
+            agg[bit + 1, c, rows] = (
+                jnp.exp(their_total) * agg[bit, c, rows] + from_tok[bit, c, rows]
+            )
 
         if bit + 1 < tok_bits:
-            tok_copy(bit + 1, c).start()
+            tok_copy(bit + 1, c, part).start()
+        elif seq_bits:
+
+            @pl.when(sends_own)
+            def _():
+                if c == 0 and part == 0:
+                    seq_copy(agg_total.at[tok_bits], 0, chunks).start()
+                seq_copy(agg.at[tok_bits, c], 0, c, part).start()
 
     def tok_totals(bit):
         tok_copy(bit, chunks).wait_recv()
@@ -296,27 +316,6 @@
         def _():
             far(near_levels + 1 + bit, from_tok.at[bit, c], row_of(pref.at[bit], c), c)
 
-    sends_own = jnp.logical_and(has_next, trailing[0]) if seq_bits else None
-    pref[0] = jnp.zeros(pref.shape[1:], F32)
-    for bit in range(max(tok_bits, 1)):
-        for c in range(chunks):
-            if bit == 0:
-                near(c)
-            if bit < tok_bits:
-                if c == 0:
-                    tok_totals(bit)
-                tok_step(bit, c)
-            if bit + 1 >= tok_bits and seq_bits:
-
-                @pl.when(sends_own)
-                def _():
-                    if c == 0:
-                        seq_copy(agg_total.at[tok_bits], 0, chunks).start()
-                    seq_copy(agg.at[tok_bits, c], 0, c).start()
-
-            if bit < tok_bits:
-                tok_read(bit, c)
-
     def held(slot):
         return ((seq >> slot) & 1) == 1
 
@@ -357,18 +356,19 @@
         def _():
             seq_copy(agg.at[tok_bits, c], slot, c).wait_recv()
 
-            @pl.when(forwards(slot))
-            def _():
-                seq_copy(from_seq.at[slot, c], slot, c).start()
-
-            if splits(slot):
+            if slot:
+
+                @pl.when(forwards(slot))
+                def _():
+                    seq_copy(from_seq.at[slot, c], slot, c).start()
+
                 swap_copy(slot, c, mine_at).start()
 
             if slot + 1 < seq_bits:
 
                 @pl.when(chains(slot + 1))
                 def _():
-                    rows = pl.ds(mine_at, half) if splits(slot + 1) else slice(None)
+                    rows = rows_of(0)
                     total = row_of(agg_total.at[tok_bits], c)
                     state = agg[tok_bits, c, rows]
                     for lower in range(slot + 1):
@@ -380,8 +380,10 @@
     def seq_read(slot, c):
         @pl.when(held(slot))
         def _():
-            if splits(slot):
+            if slot:
                 swap_copy(slot, c, other_at).wait_recv()
+            else:
+                seq_copy(agg.at[tok_bits, c], 0, c, 1).wait_recv()
             far(
                 near_levels + 1 + tok_bits + slot,
                 from_seq.at[slot, c],
@@ -398,32 +400,56 @@
         mean = mm((y * y).astype(BF16), same_head) * (1.0 / head_size)
         o_ref[:, cols(c)] = y * lax.rsqrt(mean + 1e-5)
 
+    pref[0] = jnp.zeros(pref.shape[1:], F32)
+    lag = min(2, chunks - 1)
+    last = tok_bits - 1
+    for bit in range(tok_bits):
+        for c in range(chunks):
+            if bit == 0:
+                near(c)
+            if c == 0:
+                tok_totals(bit)
+            tok_step(bit, c, 0)
+            if bit == last and seq_bits and c >= lag:
+                if c == lag:
+                    seq_totals(0)
+                seq_step(0, c - lag)
+    for bit in range(last):
+        for c in range(chunks):
+            tok_step(bit, c, 1)
+            tok_read(bit, c)
+    for c in range(chunks + 1):
+        if c < chunks:
+            if seq_bits and c + chunks - lag < chunks:
+                seq_step(0, c + chunks - lag)
+            tok_step(last, c, 1)
+            for slot in range(1, seq_bits):
+                if c == 0:
+                    seq_totals(slot)
+                seq_step(slot, c)
+            tok_read(last, c)
+            if seq_bits:
+                seq_read(0, c)
+        if c > 0:
+            for slot in range(1, seq_bits):
+                seq_read(slot, c - 1)
+            norm(c - 1)
+
+    for bit in range(tok_bits):
+        tok_copy(bit, chunks).wait_send()
+        for c in range(chunks):
+            for part in range(2):
+                tok_copy(bit, c, part).wait_send()
     for slot in range(seq_bits):
-        behind = 1 if splits(slot) else 0
-        seq_totals(slot)
-        for c in range(chunks + behind):
-            if c < chunks:
-                seq_step(slot, c)
-            if c >= behind:
-                seq_read(slot, c - behind)
-                if slot == seq_bits - 1:
-                    norm(c - behind)
-    if not seq_bits:
-        for c in range(chunks):
-            norm(c)
-
-    for bit in range(tok_bits):
-        for c in range(chunks + 1):
-            tok_copy(bit, c).wait_send()
-    for slot in range(seq_bits):
 
         @pl.when(jnp.logical_and(has_next, (((seq + 1) >> slot) & 1) == 1))
         def _():
-            for c in range(chunks + 1):
-                source = seq_total.at[slot] if c == chunks else from_seq.at[slot, c]
-                seq_copy(source, slot, c).wait_send()
-
-        if splits(slot):
+            seq_copy(seq_total.at[slot], slot, chunks).wait_send()
+            for c in range(chunks):
+                for part in range(1 if slot else 2):
+                    seq_copy(from_seq.at[slot, c], slot, c, part).wait_send()
+
+        if slot:
 
             @pl.when(held(slot))
             def _():
@@ -440,6 +466,7 @@
     chunks = columns // chunk
     tok_bits = lax.axis_size("tok").bit_length() - 1
     seq_bits = lax.axis_size("seq").bit_length() - 1
+    assert tok_bits > 0
     near_levels = (tokens // BUCKET).bit_length() - 1
     per_group = 128 // (2 * heads)
     groups = -(-(near_levels + 1) // per_group) - (
@@ -475,15 +502,15 @@
             pltpu.VMEM((tok_slots,) + totals, F32),
             pltpu.VMEM((seq_slots,) + totals, F32),
             pltpu.VMEM(totals, F32),
-            pltpu.SemaphoreType.DMA((tok_slots, chunks + 1)),
-            pltpu.SemaphoreType.DMA((tok_slots, chunks + 1)),
-            pltpu.SemaphoreType.DMA((seq_slots, chunks + 1)),
-            pltpu.SemaphoreType.DMA((seq_slots, chunks + 1)),
+            pltpu.SemaphoreType.DMA((tok_slots, 2 * chunks + 1)),
+            pltpu.SemaphoreType.DMA((tok_slots, 2 * chunks + 1)),
+            pltpu.SemaphoreType.DMA((seq_slots, 2 * chunks + 1)),
+            pltpu.SemaphoreType.DMA((seq_slots, 2 * chunks + 1)),
             pltpu.SemaphoreType.DMA((seq_slots, chunks)),
             pltpu.SemaphoreType.DMA((seq_slots, chunks)),
         ],
         compiler_params=pltpu.CompilerParams(
-            collective_id=0, has_side_effects=True, vmem_limit_bytes=40 * 2**20
+            collective_id=0, has_side_effects=True, vmem_limit_bytes=60000000
         ),
     )(values, key_rows, query_rows, decay_codes, weight_codes)
     return (normed * norm_gain[None, :]).astype(values.dtype)

time: 39.2 us -> 32.7 us (0.83)
  local copies, waits for them, and re-layouts: 4.79 us -> 0.01 us
  Pallas kernels: 32.9 us -> 29.8 us
  other arithmetic: 1.23 us -> 2.82 us
    unnamed x12 -> x2, local copies, waits for them, and re-layouts: 4.79 us -> 0.01 us
    pallas_call x1, Pallas kernels: 32.9 us -> 29.8 us  [local(): pl.pallas_call(functools.partial(kernel, (tok_bits, seq_bits, head_size,...]
    convert_element_type x1, other arithmetic: 1.23 us -> 2.82 us  [local(): return (normed * norm_gain[None, :]).astype(values.dtype)]
where the time goes in v3:
time: 32.7 us; the launch traced here: 32.6 us
  Pallas kernels  29.8 us (91%)
  other arithmetic  2.82 us (9%)
    pallas_call x1, Pallas kernels, local(): pl.pallas_call(functools.partial(kernel, (tok_bits, seq_bits, head_size,...  29.8 us
    convert_element_type x1, other arithmetic, local(): return (normed * norm_gain[None, :]).astype(values.dtype)  2.82 us

profile of v3, /device:TPU:24, one launch (start us, length us, event | category | flops | bytes accessed | tf_op | source)
XLA Modules:
  0.0 32.6 jit_solution(14276051878937677290)
XLA Ops:
  0.0 0.0 copy-start
  0.0 29.8 %shard_map.64 = f32[512,1024]{1,0:T(8,128)} custom-call(bf16[512,1024]{1,0:T(8,128)(2,1)} %v_hbm.1, bf16[512,128]{1,0:T(8,128)(2,1)} %k_hbm.1, bf16[512,128]{1,0:T(8,128)(2,1)} %q_hbm.1, s32[16,512]{1,0:T(8,128)} %codes_hbm.1, s32[12,16,512]{2,1,0:T(8,128)} %w_hbm.1), custom_call_target="tpu_custom_call" | custom-call | tf_op jit(solution)/shard_map/pallas_call | solution.py:479
  29.8 0.0 copy-done
  29.8 2.8 %multiply_convert_fusion = bf16[512,1024]{1,0:T(8,128)(2,1)} fusion(f32[512,1024]{1,0:T(8,128)} %shard_map.64, f32[1024]{0:T(1024)S(1)} %copy-done), kind=kLoop, calls=%fused_computation | loop fusion | flops 1048576 | bytes 3149824 | tf_op jit(solution)/shard_map/convert_element_type | solution.py:516
Async XLA Ops:
  0.0 29.8 %copy-start = (f32[1024]{0:T(1024)S(1)}, f32[1024]{0:T(1024)}, u32[]{:S(2)}) copy-start(f32[1024]{0:T(1024)} %param.11) | copy-start | bytes 12292

commit v4 on v3

--- a/solution.py
+++ b/solution.py
@@ -73,6 +73,9 @@
     def rows_of(part):
         return pl.ds(mine_at if part == 0 else other_at, half)
 
+    def swaps(slot, c):
+        return slot > 0 or c == 0
+
     def tok_copy(bit, c, part=0):
         if c == chunks:
             source, target = agg_total.at[bit], tok_total.at[bit]
@@ -128,6 +131,16 @@
     def cols(c):
         return slice(c * chunk, (c + 1) * chunk)
 
+    head_shift = head_size.bit_length() - 1
+    item_shift = (2 * heads).bit_length() - 1
+
+    def put_sel(i):
+        row = lax.broadcasted_iota(jnp.int32, (LANES, columns), 0)
+        column_head = lax.broadcasted_iota(jnp.int32, (LANES, columns), 1) >> head_shift
+        wanted = ((row >> item_shift) == i) & ((row & (heads - 1)) == column_head)
+        sel[i] = jnp.where(wanted, 1.0, 0.0).astype(BF16)
+
+    put_sel(0)
     load(0).wait()
     lane = lax.broadcasted_iota(jnp.int32, (heads, tokens), 1)
     run_total = codes_ref[...]
@@ -148,16 +161,6 @@
         size *= 2
     block_total = run_total.astype(F32) * (-1.0 / 65536.0)
 
-    head_shift = head_size.bit_length() - 1
-    item_shift = (2 * heads).bit_length() - 1
-
-    def put_sel(i):
-        row = lax.broadcasted_iota(jnp.int32, (LANES, columns), 0)
-        column_head = lax.broadcasted_iota(jnp.int32, (LANES, columns), 1) >> head_shift
-        wanted = ((row >> item_shift) == i) & ((row & (heads - 1)) == column_head)
-        sel[i] = jnp.where(wanted, 1.0, 0.0).astype(BF16)
-
-    put_sel(0)
     total_row = jnp.sum(
         jnp.where(
             lax.broadcasted_iota(jnp.int32, (heads, columns), 0)
@@ -295,13 +298,13 @@
 
         if bit + 1 < tok_bits:
             tok_copy(bit + 1, c, part).start()
-        elif seq_bits:
+        elif seq_bits and part == 0:
 
             @pl.when(sends_own)
             def _():
-                if c == 0 and part == 0:
+                if c == 0:
                     seq_copy(agg_total.at[tok_bits], 0, chunks).start()
-                seq_copy(agg.at[tok_bits, c], 0, c, part).start()
+                seq_copy(agg.at[tok_bits, c], 0, c, 0).start()
 
     def tok_totals(bit):
         tok_copy(bit, chunks).wait_recv()
@@ -362,6 +365,7 @@
                 def _():
                     seq_copy(from_seq.at[slot, c], slot, c).start()
 
+            if swaps(slot, c):
                 swap_copy(slot, c, mine_at).start()
 
             if slot + 1 < seq_bits:
@@ -380,7 +384,7 @@
     def seq_read(slot, c):
         @pl.when(held(slot))
         def _():
-            if slot:
+            if swaps(slot, c):
                 swap_copy(slot, c, other_at).wait_recv()
             else:
                 seq_copy(agg.at[tok_bits, c], 0, c, 1).wait_recv()
@@ -427,6 +431,12 @@
                 if c == 0:
                     seq_totals(slot)
                 seq_step(slot, c)
+            if seq_bits and not swaps(0, c):
+
+                @pl.when(sends_own)
+                def _():
+                    seq_copy(agg.at[tok_bits, c], 0, c, 1).start()
+
             tok_read(last, c)
             if seq_bits:
                 seq_read(0, c)
@@ -446,14 +456,13 @@
         def _():
             seq_copy(seq_total.at[slot], slot, chunks).wait_send()
             for c in range(chunks):
-                for part in range(1 if slot else 2):
+                for part in range(1 if swaps(slot, c) else 2):
                     seq_copy(from_seq.at[slot, c], slot, c, part).wait_send()
 
-        if slot:
-
-            @pl.when(held(slot))
-            def _():
-                for c in range(chunks):
+        @pl.when(held(slot))
+        def _():
+            for c in range(chunks):
+                if swaps(slot, c):
                     swap_copy(slot, c, mine_at).wait_send()
 
 
@@ -473,6 +482,7 @@
         -(near_levels + 1 + tok_bits + seq_bits) // per_group
     )
     parcel = (chunks, states, chunk)
+    arrays = (values, key_rows, query_rows, decay_codes, weight_codes)
     totals = (columns // LANES, LANES)
     tok_slots, seq_slots = max(tok_bits, 1), max(seq_bits, 1)
     vmem = pl.BlockSpec(memory_space=pltpu.VMEM)
@@ -484,7 +494,7 @@
         scratch_shapes=[
             *(
                 pltpu.VMEM(x.shape, x.dtype)
-                for x in (values, key_rows, query_rows, decay_codes, weight_codes)
+                for x in arrays
             ),
             pltpu.SemaphoreType.DMA((5,)),
             pltpu.VMEM((tokens, columns), F32),
@@ -510,9 +520,9 @@
             pltpu.SemaphoreType.DMA((seq_slots, chunks)),
         ],
         compiler_params=pltpu.CompilerParams(
-            collective_id=0, has_side_effects=True, vmem_limit_bytes=60000000
+            collective_id=0, has_side_effects=True, vmem_limit_bytes=40 * 2**20
         ),
-    )(values, key_rows, query_rows, decay_codes, weight_codes)
+    )(*(pltpu.with_memory_space_constraint(x, pltpu.HBM) for x in arrays))
     return (normed * norm_gain[None, :]).astype(values.dtype)
 
 

time: 32.7 us -> 28.7 us (0.88)
  Pallas kernels: 29.8 us -> 27.3 us
  other arithmetic: 2.82 us -> 1.23 us
    pallas_call x1, Pallas kernels: 29.8 us -> 27.3 us  [local(): pl.pallas_call(functools.partial(kernel, (tok_bits, seq_bits, head_size,...]
    convert_element_type x1, other arithmetic: 2.82 us -> 1.23 us  [local(): return (normed * norm_gain[None, :]).astype(values.dtype)]
where the time goes in v4:
time: 28.7 us; the launch traced here: 28.6 us
  Pallas kernels  27.3 us (95%)
  other arithmetic  1.23 us (4%)
    pallas_call x1, Pallas kernels, local(): pl.pallas_call(functools.partial(kernel, (tok_bits, seq_bits, head_size,...  27.3 us
    convert_element_type x1, other arithmetic, local(): return (normed * norm_gain[None, :]).astype(values.dtype)  1.23 us

profile of v4, /device:TPU:24, one launch (start us, length us, event | category | flops | bytes accessed | tf_op | source)
XLA Modules:
  0.0 28.6 jit_solution(18226541144077290612)
XLA Ops:
  0.0 0.0 copy-start
  0.0 27.3 %shard_map.64 = f32[512,1024]{1,0:T(8,128)S(1)} custom-call(bf16[512,1024]{1,0:T(8,128)(2,1)} %v_hbm.1, bf16[512,128]{1,0:T(8,128)(2,1)} %k_hbm.1, bf16[512,128]{1,0:T(8,128)(2,1)} %q_hbm.1, s32[16,512]{1,0:T(8,128)} %codes_hbm.1, s32[12,16,512]{2,1,0:T(8,128)} %w_hbm.1), custom_call_target="tpu_custom_call" | custom-call | tf_op jit(solution)/shard_map/pallas_call | solution.py:489
  27.3 0.0 copy-done
  27.3 1.2 %multiply_convert_fusion = bf16[512,1024]{1,0:T(8,128)(2,1)} fusion(f32[512,1024]{1,0:T(8,128)S(1)} %shard_map.64, f32[1024]{0:T(1024)S(1)} %copy-done), kind=kLoop, calls=%fused_computation | loop fusion | flops 1048576 | bytes 3149824 | tf_op jit(solution)/shard_map/convert_element_type | solution.py:526
Async XLA Ops:
  0.0 27.3 %copy-start = (f32[1024]{0:T(1024)S(1)}, f32[1024]{0:T(1024)}, u32[]{:S(2)}) copy-start(f32[1024]{0:T(1024)} %param.11) | copy-start | bytes 12292

commit v5 on v4

--- a/solution.py
+++ b/solution.py
@@ -74,7 +74,7 @@
         return pl.ds(mine_at if part == 0 else other_at, half)
 
     def swaps(slot, c):
-        return slot > 0 or c == 0
+        return slot > 0 or c in (0, 2)
 
     def tok_copy(bit, c, part=0):
         if c == chunks:
@@ -405,7 +405,7 @@
         o_ref[:, cols(c)] = y * lax.rsqrt(mean + 1e-5)
 
     pref[0] = jnp.zeros(pref.shape[1:], F32)
-    lag = min(2, chunks - 1)
+    lag = min(1, chunks - 1)
     last = tok_bits - 1
     for bit in range(tok_bits):
         for c in range(chunks):

time: 28.7 us -> 27.9 us (0.972)
  Pallas kernels: 27.3 us -> 26.5 us
    pallas_call x1, Pallas kernels: 27.3 us -> 26.5 us  [local(): pl.pallas_call(functools.partial(kernel, (tok_bits, seq_bits, head_size,...]
where the time goes in v5:
time: 27.9 us; the launch traced here: 27.7 us
  Pallas kernels  26.5 us (95%)
  other arithmetic  1.23 us (4%)
    pallas_call x1, Pallas kernels, local(): pl.pallas_call(functools.partial(kernel, (tok_bits, seq_bits, head_size,...  26.5 us
    convert_element_type x1, other arithmetic, local(): return (normed * norm_gain[None, :]).astype(values.dtype)  1.23 us

profile of v5, /device:TPU:24, one launch (start us, length us, event | category | flops | bytes accessed | tf_op | source)
XLA Modules:
  0.0 27.7 jit_solution(933298986768749425)
XLA Ops:
  0.0 0.0 copy-start
  0.0 26.5 %shard_map.64 = f32[512,1024]{1,0:T(8,128)S(1)} custom-call(bf16[512,1024]{1,0:T(8,128)(2,1)} %v_hbm.1, bf16[512,128]{1,0:T(8,128)(2,1)} %k_hbm.1, bf16[512,128]{1,0:T(8,128)(2,1)} %q_hbm.1, s32[16,512]{1,0:T(8,128)} %codes_hbm.1, s32[12,16,512]{2,1,0:T(8,128)} %w_hbm.1), custom_call_target="tpu_custom_call" | custom-call | tf_op jit(solution)/shard_map/pallas_call | solution.py:489
  26.5 0.0 copy-done
  26.5 1.2 %multiply_convert_fusion = bf16[512,1024]{1,0:T(8,128)(2,1)} fusion(f32[512,1024]{1,0:T(8,128)S(1)} %shard_map.64, f32[1024]{0:T(1024)S(1)} %copy-done), kind=kLoop, calls=%fused_computation | loop fusion | flops 1048576 | bytes 3149824 | tf_op jit(solution)/shard_map/convert_element_type | solution.py:526
Async XLA Ops:
  0.0 26.5 %copy-start = (f32[1024]{0:T(1024)S(1)}, f32[1024]{0:T(1024)}, u32[]{:S(2)}) copy-start(f32[1024]{0:T(1024)} %param.11) | copy-start | bytes 12292
